TPU v7x, 32 devices: a whole 2x2x4 slice. The times are simulated.
32 devices in a mesh: cache: 8 (over z, x), owner: 4 (over y, core).
Axes of the slice: x: 2, y: 2, z: 4, core: 2. Of those that a mesh axis runs over, the one named last changes fastest.
Arguments:
- cache: bfloat16 [32, 4, 128, 256], P('cache'), may hold values from -2.5 to 2.5
- backing: bfloat16 [32, 32, 128, 256], P('cache', 'owner'), may hold values from -2.5 to 2.5
- resident: int32 [32, 4], P('cache'), may hold values from 0 to 31, as said below
- promote: int32 [32, 2], P('cache'), may hold values from 0 to 31, as said below
- victim: int32 [32, 2], P('cache'), may hold values from 0 to 3, as said below
- lookups: int32 [2, 4096, 32, 8], P(None, 'owner', 'cache'), may hold values from 0 to 511
- route: int32 [2, 4, 1024], P(None, 'owner'), may hold values from 0 to 1023, each once within a row
- dcn_down: bfloat16 [8192, 128], P('cache'), may hold values from -0.0625 to 0.0625
- dcn_up: bfloat16 [128, 8192], P(None, 'cache'), may hold values from -0.5 to 0.5
- dcn_bias: float32 [8192], replicated, may hold values from -5 to 5
- mlp_in: bfloat16 [8192, 1024], P('cache'), may hold values from -0.0625 to 0.0625
- mlp_bias: float32 [1024], replicated, may hold values from -3 to 3
- mlp_out: float32 [1024], replicated, may hold values from -0.1875 to 0.1875
- out_bias: float32 [1], replicated, may hold values from -4 to 4
Outputs:
- scores: float32 [2, 4, 1024], P(None, 'owner', 'cache')
- new_cache: bfloat16 [32, 4, 128, 256], P('cache')
- new_backing: bfloat16 [32, 32, 128, 256], P('cache', 'owner')
Inputs may be any that keep to these rules, and one draw needn't show every extreme that they name: `resident`: for each feature, 4 distinct backing blocks. `promote`: for each feature, 2 distinct backing blocks, none of them in that feature's resident; block k belongs to owner k // 8. `victim`: for each feature, 2 distinct slots. `route`: each batch and owner group holds every request index once.
All inputs are finite; a program needn't handle non-finite values.
Results may differ from a plain program's by a relative error of at most 0.004.
Values may be sent and summed in bfloat16 or wider, within the bound.
A program may use at most 128 MiB of HBM per device.

v0:
```python
import jax
import jax.numpy as jnp
from jax import lax
from jax.sharding import PartitionSpec as P


def take_rows(table, wanted):
    return jax.vmap(lambda rows, chosen: rows[chosen])(table, wanted)


def pool_batch(requests, order, table):
    requests = requests[order]
    count = requests.shape[0]
    step = min(512, count)
    codes = jnp.arange(table.shape[1], dtype=jnp.int32)

    def one_block(lookup_block):
        counts = jnp.sum((lookup_block[..., None] == codes).astype(jnp.bfloat16), axis=2)
        return jnp.einsum("rfk,fke->rfe", counts, table, preferred_element_type=jnp.float32).astype(
            jnp.bfloat16
        )

    blocks = requests.reshape((count // step, step) + requests.shape[1:])
    pooled = lax.map(one_block, blocks)
    return pooled.reshape((count,) + pooled.shape[2:])


def on_device(
    cache,
    backing,
    resident,
    promote,
    victim,
    lookups,
    route,
    dcn_down,
    dcn_up,
    dcn_bias,
    mlp_in,
    mlp_bias,
    mlp_out,
    out_bias,
):
    held = cache.shape[0]
    slots = cache.shape[1]
    block = cache.shape[2]
    width = cache.shape[3]
    own_blocks = backing.shape[1]
    promoted_count = promote.shape[1]
    owner_here = lax.axis_index("owner")
    local_index = promote - owner_here * own_blocks
    owned_here = (local_index >= 0) & (local_index < own_blocks)
    clamped = jnp.clip(local_index, 0, own_blocks - 1)
    fetched = take_rows(backing, clamped)
    outgoing = jnp.where(owned_here[:, :, None, None], fetched, jnp.zeros_like(fetched))
    arrived = lax.all_gather(outgoing, "owner", axis=0, tiled=True)
    owners = arrived.shape[0] // held
    arrived = arrived.reshape(owners, held, promoted_count, block, width)
    source = promote // own_blocks
    picked = source[None] == jnp.arange(owners, dtype=jnp.int32)[:, None, None]
    promoted = jnp.sum(jnp.where(picked[..., None, None], arrived, jnp.zeros_like(arrived)), axis=0)
    evicted = take_rows(cache, victim)
    leaving = take_rows(resident, victim) - owner_here * own_blocks
    slot_numbers = jnp.arange(slots, dtype=jnp.int32)
    block_numbers = jnp.arange(own_blocks, dtype=jnp.int32)
    new_cache = cache
    new_backing = backing
    for column in range(promoted_count):
        slot_hit = victim[:, column][:, None] == slot_numbers[None, :]
        new_cache = jnp.where(slot_hit[:, :, None, None], promoted[:, column][:, None], new_cache)
        block_hit = leaving[:, column][:, None] == block_numbers[None, :]
        new_backing = jnp.where(
            block_hit[:, :, None, None], evicted[:, column][:, None], new_backing
        )
    table = new_cache.reshape(held, slots * block, width)
    batches = lookups.shape[0]
    received = []
    for batch_turn in range(batches):
        pooled = pool_batch(lookups[batch_turn], route[batch_turn, 0], table)
        received.append(lax.all_to_all(pooled, "cache", split_axis=0, concat_axis=1, tiled=True))
    arrived_rows = jnp.stack(received)
    per_batch = arrived_rows.shape[1]
    features = arrived_rows.reshape(batches * per_batch, -1)
    low = jnp.dot(
        features,
        lax.all_gather(dcn_down, "cache", axis=0, tiled=True),
        preferred_element_type=jnp.float32,
    ).astype(jnp.bfloat16)
    gate = (
        jnp.dot(
            low,
            lax.all_gather(dcn_up, "cache", axis=1, tiled=True),
            preferred_element_type=jnp.float32,
        )
        + dcn_bias
    )
    crossed = (features * gate + features).astype(jnp.bfloat16)
    portion = mlp_in.shape[1] // lax.axis_size("owner")
    own_columns = lax.dynamic_slice_in_dim(mlp_in, owner_here * portion, portion, 1)
    column_block = lax.all_gather(own_columns, "cache", axis=0, tiled=True)
    before = jnp.dot(
        crossed,
        lax.all_gather(column_block, "owner", axis=1, tiled=True),
        preferred_element_type=jnp.float32,
    )
    hidden = jnp.maximum(before + mlp_bias, 0.0)
    scores = jnp.sum(hidden * mlp_out, axis=-1) + out_bias[0]
    return (scores.reshape(batches, 1, per_batch), new_cache, new_backing)


def solution(mesh):
    in_specs = (
        P("cache", None, None, None),
        P("cache", "owner", None, None),
        P("cache", None),
        P("cache", None),
        P("cache", None),
        P(None, "owner", "cache", None),
        P(None, "owner", None),
        P("cache", None),
        P(None, "cache"),
        P(),
        P("cache", None),
        P(),
        P(),
        P(),
    )
    out_specs = (
        P(None, "owner", "cache"),
        P("cache", None, None, None),
        P("cache", "owner", None, None),
    )
    return jax.shard_map(
        on_device, mesh=mesh, in_specs=in_specs, out_specs=out_specs, check_vma=False
    )
```

profile of v0, /device:TPU:0, one launch (start us, length us, event | category | flops | bytes accessed | tf_op | source)
XLA Modules:
  0.0 392.6 jit_solution(9065323531690684591)
XLA Ops:
  7.2 1.5 copy-done
  8.8 0.9 constant_dynamic-slice_fusion
  9.7 0.7 fusion.37
  10.6 0.7 compare_and_fusion
  11.4 2.2 gather_fusion.2
  13.6 0.9 broadcast_select_fusion
  14.5 0.7 all-gather.8.cloned.1.call-update
  15.8 70.4 %all-gather.12.cloned.1.call-done = bf16[8192,256]{1,0:T(8,128)(2,1)} async-done(((bf16[1024,256]{1,0:T(8,128)(2,1)}), bf16[8192,256]{1,0:T(8,128)(2,1)}) %all-gather.12.cloned.1.call-update) | async-done | bytes 4194320 | tf_op jit(solution)/shard_map/all_gather | solution.py:100
  86.3 0.6 copy-done.9
  87.2 0.8 copy.137
  88.1 7.9 %gather_fusion = s32[1024,4,8]{2,1,0:T(4,128)} fusion(s32[1024,4,8]{2,1,0:T(4,128)S(1)} %bitcast.100, s32[1024]{0:T(1024)S(1)} %broadcast_clamp_fusion.1), kind=kCustom, calls=%fused_computation | custom fusion | bytes 266240 | tf_op jit(solution)/shard_map/gather | solution.py:12
  96.0 1.8 copy.113
  98.0 10.9 %all-gather.6.cloned.1.call-done = bf16[16,2,128,256]{3,2,1,0:T(8,128)(2,1)} async-done(((bf16[4,2,128,256]{3,2,1,0:T(8,128)(2,1)}), bf16[16,2,128,256]{3,2,1,0:T(8,128)(2,1)}) %all-gather.6.cloned.1.call-update) | async-done | bytes 2097168 | tf_op jit(solution)/shard_map/all_gather | solution.py:56
  108.9 2.1 select_reduce_fusion
  111.1 1.2 select_select_fusion.1
  112.3 1.5 broadcast.130.clone2.1
  113.7 27.7 %while.26 = (s32[]{:T(128)}, bf16[2,512,4,256]{3,1,0,2:T(8,128)(2,1)}, s32[2,512,4,8]{1,3,2,0:T(8,128)S(1)}, bf16[4,512,256]{2,1,0:T(8,128)(2,1)}, s32[]{:T(128)}) while((s32[]{:T(128)}, bf16[2,512,4,256]{3,1,0,2:T(8,128)(2,1)}, s32[2,512,4,8]{1,3,2,0:T(8,128)S(1)}, bf16[4,512,256]{2,1,0:T(8,128)(2,1)}, s32[]{:T(128)}) %tuple.91), condition=%wide.region_3.4_spmd.clone, body=%wide.region_1.3_spmd.clone.sunk | while | flops 561512448 | bytes 10814045 | solution.py:24
  114.2 11.7 %fusion.60 = bf16[512,4,512]{2,1,0:T(4,128)(2,1)S(1)} fusion(s32[512,4,8]{2,1,0:T(4,128)S(1)} %copy.164), kind=kLoop, calls=%fused_computation.9.clone.1 | loop fusion | flops 24117248 | bytes 2162688 | tf_op jit(solution)/shard_map/while/body/eval_jaxpr/reduce_sum | solution.py:18
  125.9 1.7 fusion.61
  128.0 11.7 %fusion.60 = bf16[512,4,512]{2,1,0:T(4,128)(2,1)S(1)} fusion(s32[512,4,8]{2,1,0:T(4,128)S(1)} %copy.164), kind=kLoop, calls=%fused_computation.9.clone.1 | loop fusion | flops 24117248 | bytes 2162688 | tf_op jit(solution)/shard_map/while/body/eval_jaxpr/reduce_sum | solution.py:18
  139.8 1.7 fusion.61
  141.5 4.5 %copy.115 = bf16[1024,4,256]{2,1,0:T(4,128)(2,1)} copy(bf16[1024,4,256]{2,0,1:T(8,128)(2,1)} %bitcast.12) | data formatting | bytes 4194304 | tf_op jit(solution)/shard_map/reshape | solution.py:25
  146.0 5.5 %all-to-all-start = ((bf16[1024,4,256]{2,1,0:T(4,128)(2,1)}), bf16[1024,4,256]{2,1,0:T(4,128)(2,1)}, u32[]{:S(2)}, u32[]{:S(2)}) async-start(bf16[1024,4,256]{2,1,0:T(4,128)(2,1)} %copy.115), calls=%async_computation | async-start | bytes 4194304 | tf_op jit(solution)/shard_map/all_to_all | solution.py:80
  151.5 0.8 copy.138
  152.3 7.9 %gather_fusion.1 = s32[1024,4,8]{2,1,0:T(4,128)} fusion(s32[1024,4,8]{2,1,0:T(4,128)S(1)} %bitcast.101, s32[1024]{0:T(1024)S(1)} %broadcast_clamp_fusion), kind=kCustom, calls=%fused_computation.1 | custom fusion | bytes 266240 | tf_op jit(solution)/shard_map/gather | solution.py:12
  160.3 1.8 copy.120
  162.1 1.5 broadcast.130.clone2
  163.6 27.7 %while.27 = (s32[]{:T(128)}, bf16[2,512,4,256]{3,1,0,2:T(8,128)(2,1)}, s32[2,512,4,8]{1,3,2,0:T(8,128)S(1)}, bf16[4,512,256]{2,1,0:T(8,128)(2,1)}, s32[]{:T(128)}) while((s32[]{:T(128)}, bf16[2,512,4,256]{3,1,0,2:T(8,128)(2,1)}, s32[2,512,4,8]{1,3,2,0:T(8,128)S(1)}, bf16[4,512,256]{2,1,0:T(8,128)(2,1)}, s32[]{:T(128)}) %tuple.92), condition=%wide.region_6.7_spmd.clone, body=%wide.region_4.6_spmd.clone.sunk | while | flops 561512448 | bytes 10814045 | solution.py:24
  164.0 11.7 %fusion.64 = bf16[512,4,512]{2,1,0:T(4,128)(2,1)S(1)} fusion(s32[512,4,8]{2,1,0:T(4,128)S(1)} %copy.166), kind=kLoop, calls=%fused_computation.18.clone.1 | loop fusion | flops 24117248 | bytes 2162688 | tf_op jit(solution)/shard_map/while/body/eval_jaxpr/reduce_sum | solution.py:18
  175.7 1.7 fusion.65
  177.9 11.7 %fusion.64 = bf16[512,4,512]{2,1,0:T(4,128)(2,1)S(1)} fusion(s32[512,4,8]{2,1,0:T(4,128)S(1)} %copy.166), kind=kLoop, calls=%fused_computation.18.clone.1 | loop fusion | flops 24117248 | bytes 2162688 | tf_op jit(solution)/shard_map/while/body/eval_jaxpr/reduce_sum | solution.py:18
  189.6 1.7 fusion.65
  191.3 4.6 %copy.122 = bf16[1024,4,256]{2,1,0:T(4,128)(2,1)} copy(bf16[1024,4,256]{2,0,1:T(8,128)(2,1)} %bitcast.20) | data formatting | bytes 4194304 | tf_op jit(solution)/shard_map/reshape | solution.py:25
  195.9 17.7 %all-to-all-done = bf16[1024,4,256]{2,1,0:T(4,128)(2,1)} async-done(((bf16[1024,4,256]{2,1,0:T(4,128)(2,1)}), bf16[1024,4,256]{2,1,0:T(4,128)(2,1)}, u32[]{:S(2)}, u32[]{:S(2)}) %all-to-all-start) | async-done | bytes 2097184 | tf_op jit(solution)/shard_map/all_to_all | solution.py:80
  213.6 4.6 %all-to-all-start.1 = ((bf16[1024,4,256]{2,1,0:T(4,128)(2,1)}), bf16[1024,4,256]{2,1,0:T(4,128)(2,1)}, u32[]{:S(2)}, u32[]{:S(2)}) async-start(bf16[1024,4,256]{2,1,0:T(4,128)(2,1)} %copy.122), calls=%async_computation.1 | async-start | bytes 4194304 | tf_op jit(solution)/shard_map/all_to_all | solution.py:80
  219.0 0.6 gather_fusion.4
  219.6 0.7 gather_fusion.3
  220.7 3.3 select_select_fusion
  224.0 1.9 copy.116
  225.8 1.6 copy.117
  227.4 53.9 %all-to-all-done.1 = bf16[1024,4,256]{2,1,0:T(4,128)(2,1)} async-done(((bf16[1024,4,256]{2,1,0:T(4,128)(2,1)}), bf16[1024,4,256]{2,1,0:T(4,128)(2,1)}, u32[]{:S(2)}, u32[]{:S(2)}) %all-to-all-start.1) | async-done | bytes 2097184 | tf_op jit(solution)/shard_map/all_to_all | solution.py:80
  281.3 1.9 copy.123
  283.4 1.5 copy-done.3
  285.3 2.4 copy.125
  287.7 6.3 %copy.142 = bf16[32,8,32,256]{3,1,2,0:T(8,128)(2,1)} copy(bf16[32,8,32,256]{3,2,1,0:T(8,128)(2,1)S(1)} %bitcast.99) | data formatting | bytes 8388608
  294.0 4.3 %convolution_convert_fusion = bf16[256,128]{1,0:T(8,128)(2,1)S(1)} fusion(bf16[256,8192]{1,0:T(8,128)(2,1)} %bitcast.97, bf16[8192,128]{1,0:T(8,128)(2,1)} %all-gather.8.cloned.1.call-done), kind=kOutput, calls=%fused_computation.35 | convolution fusion | flops 536903680 | bytes 6356992 | tf_op jit(solution)/shard_map/dot_general | solution.py:84
  298.3 74.4 %all-gather.14.cloned.1.call-done = bf16[8192,1024]{1,0:T(8,128)(2,1)} async-done(((bf16[8192,256]{1,0:T(8,128)(2,1)}), bf16[8192,1024]{1,0:T(8,128)(2,1)}) %all-gather.14.cloned.1.call-update) | async-done | bytes 16777232 | tf_op jit(solution)/shard_map/all_gather | solution.py:103
  372.7 12.8 %fusion.33 = f32[256]{0:T(256)S(1)} fusion(bf16[8192,1024]{1,0:T(8,128)(2,1)} %all-gather.14.cloned.1.call-done, bf16[256,128]{1,0:T(8,128)(2,1)S(1)} %convolution_convert_fusion, bf16[128,8192]{1,0:T(8,128)(2,1)} %all-gather.10.cloned.1.call-done, bf16[256,8192]{1,0:T(8,128)(2,1)} %bitcast.98, f32[8192]{0:T(1024)S(1)} %copy-done.12, ...), kind=kOutput, calls=%fused_computation.34 | convolution fusion | flops 4843372544 | bytes 23176192 | tf_op jit(solution)/shard_map/dot_general | solution.py:101
  (74 shorter events, 4.9 us)
Async XLA Ops:
  7.2 1.6 copy-start
  7.2 79.0 %all-gather.12.cloned.1.call-start = ((), (), s32[]{:S(2)}) async-start(), calls=%async_computation.5 | async-start | bytes 4718592 | tf_op jit(solution)/shard_map/all_gather | solution.py:100
  9.6 99.3 %all-gather.6.cloned.1.call-start = ((), (), s32[]{:S(2)}) async-start(), calls=%async_computation.2 | async-start | bytes 2621440 | tf_op jit(solution)/shard_map/all_gather | solution.py:56
  14.5 279.5 %all-gather.8.cloned.1.call-start = ((), (), s32[]{:S(2)}) async-start(), calls=%async_computation.3 | async-start | bytes 2359296 | tf_op jit(solution)/shard_map/all_gather | solution.py:86
  15.2 283.1 %all-gather.10.cloned.1.call-start = ((), (), s32[]{:S(2)}) async-start(), calls=%async_computation.4 | async-start | bytes 2359296 | tf_op jit(solution)/shard_map/all_gather | solution.py:92
  15.8 356.9 %all-gather.14.cloned.1.call-start = ((), (), s32[]{:S(2)}) async-start(), calls=%async_computation.6 | async-start | bytes 20971520 | tf_op jit(solution)/shard_map/all_gather | solution.py:103
  86.2 0.7 copy-start.9
  86.2 1.0 copy-start.8
  86.3 1.8 copy-start.10
  96.0 1.9 copy-start.11
  97.9 13.2 %copy-start.4 = (bf16[4,4,128,256]{3,2,1,0:T(8,128)(2,1)S(1)}, bf16[4,4,128,256]{3,2,1,0:T(8,128)(2,1)}, u32[]{:S(2)}) copy-start(bf16[4,4,128,256]{3,2,1,0:T(8,128)(2,1)} %param.18) | copy-start | bytes 3145732
  114.2 11.7 %copy-start.6 = (bf16[4,512,256]{2,1,0:T(8,128)(2,1)S(1)}, bf16[4,512,256]{2,1,0:T(8,128)(2,1)}, u32[]{:S(2)}) copy-start(bf16[4,512,256]{2,1,0:T(8,128)(2,1)} %get-tuple-element.305) | copy-start | bytes 3145732 | tf_op jit(solution)/shard_map/while
  128.0 11.7 %copy-start.6 = (bf16[4,512,256]{2,1,0:T(8,128)(2,1)S(1)}, bf16[4,512,256]{2,1,0:T(8,128)(2,1)}, u32[]{:S(2)}) copy-start(bf16[4,512,256]{2,1,0:T(8,128)(2,1)} %get-tuple-element.305) | copy-start | bytes 3145732 | tf_op jit(solution)/shard_map/while
  146.0 67.6 %all-to-all-start = ((bf16[1024,4,256]{2,1,0:T(4,128)(2,1)}), bf16[1024,4,256]{2,1,0:T(4,128)(2,1)}, u32[]{:S(2)}, u32[]{:S(2)}) async-start(bf16[1024,4,256]{2,1,0:T(4,128)(2,1)} %copy.115), calls=%async_computation | async-start | bytes 4194304 | tf_op jit(solution)/shard_map/all_to_all | solution.py:80
  164.0 11.7 %copy-start.7 = (bf16[4,512,256]{2,1,0:T(8,128)(2,1)S(1)}, bf16[4,512,256]{2,1,0:T(8,128)(2,1)}, u32[]{:S(2)}) copy-start(bf16[4,512,256]{2,1,0:T(8,128)(2,1)} %get-tuple-element.290) | copy-start | bytes 3145732 | tf_op jit(solution)/shard_map/while
  177.8 11.7 %copy-start.7 = (bf16[4,512,256]{2,1,0:T(8,128)(2,1)S(1)}, bf16[4,512,256]{2,1,0:T(8,128)(2,1)}, u32[]{:S(2)}) copy-start(bf16[4,512,256]{2,1,0:T(8,128)(2,1)} %get-tuple-element.290) | copy-start | bytes 3145732 | tf_op jit(solution)/shard_map/while
  195.9 23.1 %copy-start.5 = (bf16[4,4,128,256]{3,2,1,0:T(8,128)(2,1)S(1)}, bf16[4,4,128,256]{3,2,1,0:T(8,128)(2,1)}, u32[]{:S(2)}) copy-start(bf16[4,4,128,256]{3,2,1,0:T(8,128)(2,1)} %param.18) | copy-start | bytes 3145732
  195.9 23.7 %copy-start.2 = (s32[4,4]{1,0:T(4,128)S(1)}, s32[4,4]{1,0:T(4,128)}, u32[]{:S(2)}) copy-start(s32[4,4]{1,0:T(4,128)} %param.20) | copy-start | bytes 196
  213.6 67.7 %all-to-all-start.1 = ((bf16[1024,4,256]{2,1,0:T(4,128)(2,1)}), bf16[1024,4,256]{2,1,0:T(4,128)(2,1)}, u32[]{:S(2)}, u32[]{:S(2)}) async-start(bf16[1024,4,256]{2,1,0:T(4,128)(2,1)} %copy.122), calls=%async_computation.1 | async-start | bytes 4194304 | tf_op jit(solution)/shard_map/all_to_all | solution.py:80
  283.2 1.6 copy-start.3
  294.0 78.7 %copy-start.12 = (f32[8192]{0:T(1024)S(1)}, f32[8192]{0:T(1024)}, u32[]{:S(2)}) copy-start(f32[8192]{0:T(1024)} %param.27) | copy-start | bytes 98308
  294.0 78.7 %copy-start.13 = (f32[1024]{0:T(1024)S(1)}, f32[1024]{0:T(1024)}, u32[]{:S(2)}) copy-start(f32[1024]{0:T(1024)} %param.30) | copy-start | bytes 12292
  294.0 78.7 %copy-start.14 = (f32[1024]{0:T(1024)S(1)}, f32[1024]{0:T(1024)}, u32[]{:S(2)}) copy-start(f32[1024]{0:T(1024)} %param.29) | copy-start | bytes 12292
  372.7 13.3 %copy-start.1 = (bf16[1024,1024]{1,0:T(8,128)(2,1)S(1)}, bf16[1024,1024]{1,0:T(8,128)(2,1)}, u32[]{:S(2)}) copy-start(bf16[1024,1024]{1,0:T(8,128)(2,1)} %param.28) | copy-start | bytes 6291460
Sparse Core Ops, SparseCore 0:
  10.7 75.4 all-gather.11
  87.8 21.0 all-gather.5
  111.1 52.2 all-gather.7
  165.3 89.3 all-gather.9
  256.1 116.5 all-gather.13
where the time goes:
time: 393 us
  waiting for transfers between devices  229 us (58%)
  local copies, waits for them, and re-layouts  58.2 us (15%)
  other arithmetic  56.9 us (14%)
  matrix products  23.8 us (6%)
  between operations  14.7 us (4%)
  starting transfers between devices  10.3 us (3%)
    all_gather x1, waiting for transfers between devices, on_device(): lax.all_gather(column_block, 'owner', axis=1, tiled=True)  74.4 us
    all_to_all x2, waiting for transfers between devices, on_device(): lax.all_to_all(pooled, 'cache', split_axis=0, concat_axis=1, tiled=True)  71.6 us
    all_gather x1, waiting for transfers between devices, on_device(): column_block = lax.all_gather(own_columns, 'cache', axis=0, tiled=True)  70.4 us
    reduce_sum x4, other arithmetic, one_block(): jnp.sum((lookup_block[..., None] == codes).astype(jnp.bfloat16), axis=2)  46.9 us
    gather x2, local copies, waits for them, and re-layouts, pool_batch(): requests = requests[order]  15.9 us
    unnamed x31, local copies, waits for them, and re-layouts  15.5 us
    dot_general x1, matrix products, on_device(): jnp.dot(crossed, lax.all_gather(column_block, 'owner', axis=1, tiled=True...  12.8 us
    all_gather x1, waiting for transfers between devices, on_device(): arrived = lax.all_gather(outgoing, 'owner', axis=0, tiled=True)  10.9 us
  transfers between devices with their start and end apart: 7, of which 5 were waited for; matrix products, arithmetic and copies ran while one was open for 31% of the time, Pallas kernels for 0%

commit v1 on v0

--- a/solution.py
+++ b/solution.py
@@ -77,7 +77,17 @@
     received = []
     for batch_turn in range(batches):
         pooled = pool_batch(lookups[batch_turn], route[batch_turn, 0], table)
-        received.append(lax.all_to_all(pooled, "cache", split_axis=0, concat_axis=1, tiled=True))
+        received.append(
+            jnp.concatenate(
+                lax.all_to_all(
+                    jnp.stack(jnp.split(pooled, lax.axis_size("cache"), 0), 0),
+                    axis_name="cache",
+                    split_axis=0,
+                    concat_axis=0,
+                ),
+                1,
+            )
+        )
     arrived_rows = jnp.stack(received)
     per_batch = arrived_rows.shape[1]
     features = arrived_rows.reshape(batches * per_batch, -1)

time: 393 us -> 364 us (0.926)
  waiting for transfers between devices: 229 us -> 186 us
  local copies, waits for them, and re-layouts: 58.2 us -> 69 us
    all_gather x1, waiting for transfers between devices: 74.4 us -> 41.3 us  [on_device(): lax.all_gather(column_block, 'owner', axis=1, tiled=True)]
    unnamed x31 -> x43, local copies, waits for them, and re-layouts: 15.5 us -> 37.6 us
    all_gather x1, waiting for transfers between devices: 10.9 us -> 0.3 us  [on_device(): arrived = lax.all_gather(outgoing, 'owner', axis=0, tiled=True)]
    reshape x2 -> x0, local copies, waits for them, and re-layouts: 9.14 us -> none  [pool_batch(): return pooled.reshape((count,) + pooled.shape[2:])]
    all_to_all x4 -> x0, local copies, waits for them, and re-layouts: 5.49 us -> none  [on_device(): lax.all_to_all(pooled, 'cache', split_axis=0, concat_axis=1, tiled=True)]
  transfers between devices with their start and end apart: 7 -> 7, of which waited for: 5 -> 5; matrix products, arithmetic and copies ran while one was open for 31% -> 37% of each run, Pallas kernels for 0% -> 0%
where the time goes in v1:
time: 364 us; the launch traced here: 363 us
  waiting for transfers between devices  186 us (51%)
  local copies, waits for them, and re-layouts  69 us (19%)
  other arithmetic  59.4 us (16%)
  matrix products  23.6 us (6%)
  between operations  14.6 us (4%)
  starting transfers between devices  10.2 us (3%)
    all_to_all x2, waiting for transfers between devices, on_device(): lax.all_to_all(jnp.stack(jnp.split(pooled, lax.axis_size('cache'), 0), 0)...  73 us
    all_gather x1, waiting for transfers between devices, on_device(): column_block = lax.all_gather(own_columns, 'cache', axis=0, tiled=True)  70.4 us
    reduce_sum x4, other arithmetic, one_block(): jnp.sum((lookup_block[..., None] == codes).astype(jnp.bfloat16), axis=2)  46.9 us
    all_gather x1, waiting for transfers between devices, on_device(): lax.all_gather(column_block, 'owner', axis=1, tiled=True)  41.3 us
    unnamed x43, local copies, waits for them, and re-layouts  37.6 us
    gather x2, local copies, waits for them, and re-layouts, pool_batch(): requests = requests[order]  15.9 us
    dot_general x1, matrix products, on_device(): jnp.dot(crossed, lax.all_gather(column_block, 'owner', axis=1, tiled=True...  12.7 us
    all_to_all x2, starting transfers between devices, on_device(): lax.all_to_all(jnp.stack(jnp.split(pooled, lax.axis_size('cache'), 0), 0)...  10 us
  transfers between devices with their start and end apart: 7, of which 5 were waited for; matrix products, arithmetic and copies ran while one was open for 37% of the time, Pallas kernels for 0%

profile of v1, /device:TPU:0, one launch (start us, length us, event | category | flops | bytes accessed | tf_op | source)
XLA Modules:
  0.0 363.3 jit_solution(2595879105080041692)
XLA Ops:
  7.2 1.5 copy-done
  11.4 2.2 gather_fusion.2
  15.8 70.4 %all-gather.12.cloned.1.call-done = bf16[8192,256]{1,0:T(8,128)(2,1)} async-done(((bf16[1024,256]{1,0:T(8,128)(2,1)}), bf16[8192,256]{1,0:T(8,128)(2,1)}) %all-gather.12.cloned.1.call-update) | async-done | bytes 4194320 | tf_op jit(solution)/shard_map/all_gather | solution.py:110
  88.1 7.9 %gather_fusion = s32[1024,4,8]{2,1,0:T(4,128)} fusion(s32[1024,4,8]{2,1,0:T(4,128)S(1)} %bitcast.162, s32[1024]{0:T(1024)S(1)} %get-tuple-element.216), kind=kCustom, calls=%fused_computation | custom fusion | bytes 266240 | tf_op jit(solution)/shard_map/gather | solution.py:12
  96.0 1.8 copy.89
  98.7 7.9 %gather_fusion.1 = s32[1024,4,8]{2,1,0:T(4,128)} fusion(s32[1024,4,8]{2,1,0:T(4,128)S(1)} %bitcast.163, s32[1024]{0:T(1024)S(1)} %get-tuple-element.215), kind=kCustom, calls=%fused_computation.1 | custom fusion | bytes 266240 | tf_op jit(solution)/shard_map/gather | solution.py:12
  106.6 1.9 copy.93
  108.9 2.1 select_reduce_fusion
  111.1 1.2 select_select_fusion.1
  112.3 1.5 broadcast.130.clone2.1
  113.7 27.7 %while.26 = (s32[]{:T(128)}, bf16[2,512,4,256]{3,1,0,2:T(8,128)(2,1)}, s32[2,512,4,8]{1,3,2,0:T(8,128)S(1)}, bf16[4,512,256]{2,1,0:T(8,128)(2,1)}, s32[]{:T(128)}) while((s32[]{:T(128)}, bf16[2,512,4,256]{3,1,0,2:T(8,128)(2,1)}, s32[2,512,4,8]{1,3,2,0:T(8,128)S(1)}, bf16[4,512,256]{2,1,0:T(8,128)(2,1)}, s32[]{:T(128)}) %tuple.90), condition=%wide.region_3.4_spmd.clone, body=%wide.region_1.3_spmd.clone.sunk | while | flops 561512448 | bytes 10814045 | solution.py:24
  114.2 11.7 %fusion.76 = bf16[512,4,512]{2,1,0:T(4,128)(2,1)S(1)} fusion(s32[512,4,8]{2,1,0:T(4,128)S(1)} %copy.134), kind=kLoop, calls=%fused_computation.9.clone.1 | loop fusion | flops 24117248 | bytes 2162688 | tf_op jit(solution)/shard_map/while/body/eval_jaxpr/reduce_sum | solution.py:18
  125.9 1.7 fusion.77
  128.0 11.7 %fusion.76 = bf16[512,4,512]{2,1,0:T(4,128)(2,1)S(1)} fusion(s32[512,4,8]{2,1,0:T(4,128)S(1)} %copy.134), kind=kLoop, calls=%fused_computation.9.clone.1 | loop fusion | flops 24117248 | bytes 2162688 | tf_op jit(solution)/shard_map/while/body/eval_jaxpr/reduce_sum | solution.py:18
  139.8 1.7 fusion.77
  141.5 1.7 fusion.49
  143.1 1.7 fusion.48
  144.8 1.7 fusion.47
  146.5 1.7 fusion.46
  148.1 1.7 fusion.45
  149.8 1.7 fusion.44
  151.5 1.7 fusion.43
  153.2 1.7 fusion.42
  154.9 5.5 %all-to-all-start = ((bf16[8,128,4,256]{3,1,2,0:T(8,128)(2,1)}), bf16[8,128,4,256]{3,1,2,0:T(8,128)(2,1)}, u32[]{:S(2)}, u32[]{:S(2)}) async-start(bf16[8,128,4,256]{3,1,2,0:T(8,128)(2,1)} %fusion.42), calls=%async_computation | async-start | bytes 4194304 | tf_op jit(solution)/shard_map/all_to_all | solution.py:82
  160.4 1.5 broadcast.130.clone2
  161.9 27.7 %while.27 = (s32[]{:T(128)}, bf16[2,512,4,256]{3,1,0,2:T(8,128)(2,1)}, s32[2,512,4,8]{1,3,2,0:T(8,128)S(1)}, bf16[4,512,256]{2,1,0:T(8,128)(2,1)}, s32[]{:T(128)}) while((s32[]{:T(128)}, bf16[2,512,4,256]{3,1,0,2:T(8,128)(2,1)}, s32[2,512,4,8]{1,3,2,0:T(8,128)S(1)}, bf16[4,512,256]{2,1,0:T(8,128)(2,1)}, s32[]{:T(128)}) %tuple.91), condition=%wide.region_6.7_spmd.clone, body=%wide.region_4.6_spmd.clone.sunk | while | flops 561512448 | bytes 10814045 | solution.py:24
  162.3 11.7 %fusion.80 = bf16[512,4,512]{2,1,0:T(4,128)(2,1)S(1)} fusion(s32[512,4,8]{2,1,0:T(4,128)S(1)} %copy.136), kind=kLoop, calls=%fused_computation.18.clone.1 | loop fusion | flops 24117248 | bytes 2162688 | tf_op jit(solution)/shard_map/while/body/eval_jaxpr/reduce_sum | solution.py:18
  174.0 1.7 fusion.81
  176.2 11.7 %fusion.80 = bf16[512,4,512]{2,1,0:T(4,128)(2,1)S(1)} fusion(s32[512,4,8]{2,1,0:T(4,128)S(1)} %copy.136), kind=kLoop, calls=%fused_computation.18.clone.1 | loop fusion | flops 24117248 | bytes 2162688 | tf_op jit(solution)/shard_map/while/body/eval_jaxpr/reduce_sum | solution.py:18
  187.9 1.7 fusion.81
  189.6 1.7 fusion.41
  191.3 1.7 fusion.40
  193.0 1.7 fusion.39
  194.6 1.7 fusion.38
  196.3 1.7 fusion.37
  198.0 1.7 fusion.36
  199.7 1.7 fusion.35
  201.3 1.7 fusion.34
  203.0 31.5 %all-to-all-done = bf16[8,128,4,256]{3,1,2,0:T(8,128)(2,1)} async-done(((bf16[8,128,4,256]{3,1,2,0:T(8,128)(2,1)}), bf16[8,128,4,256]{3,1,2,0:T(8,128)(2,1)}, u32[]{:S(2)}, u32[]{:S(2)}) %all-to-all-start) | async-done | bytes 2097184 | tf_op jit(solution)/shard_map/all_to_all | solution.py:82
  234.5 4.5 %all-to-all-start.1 = ((bf16[8,128,4,256]{3,1,2,0:T(8,128)(2,1)}), bf16[8,128,4,256]{3,1,2,0:T(8,128)(2,1)}, u32[]{:S(2)}, u32[]{:S(2)}) async-start(bf16[8,128,4,256]{3,1,2,0:T(8,128)(2,1)} %fusion.34), calls=%async_computation.1 | async-start | bytes 4194304 | tf_op jit(solution)/shard_map/all_to_all | solution.py:82
  241.5 3.6 select_select_fusion
  245.1 41.6 %all-to-all-done.1 = bf16[8,128,4,256]{3,1,2,0:T(8,128)(2,1)} async-done(((bf16[8,128,4,256]{3,1,2,0:T(8,128)(2,1)}), bf16[8,128,4,256]{3,1,2,0:T(8,128)(2,1)}, u32[]{:S(2)}, u32[]{:S(2)}) %all-to-all-start.1) | async-done | bytes 2097184 | tf_op jit(solution)/shard_map/all_to_all | solution.py:82
  286.7 2.6 pad_maximum_fusion
  289.3 2.4 copy.95
  291.7 6.3 %copy.112 = bf16[32,8,32,256]{3,1,2,0:T(8,128)(2,1)} copy(bf16[32,8,32,256]{3,2,1,0:T(8,128)(2,1)S(1)} %bitcast.161) | data formatting | bytes 8388608
  298.0 4.1 %convolution_convert_fusion = bf16[256,128]{1,0:T(8,128)(2,1)S(1)} fusion(bf16[256,8192]{1,0:T(8,128)(2,1)} %bitcast.159, bf16[8192,128]{1,0:T(8,128)(2,1)} %all-gather.8.cloned.1.call-done), kind=kOutput, calls=%fused_computation.35 | convolution fusion | flops 536903680 | bytes 6356992 | tf_op jit(solution)/shard_map/dot_general | solution.py:94
  302.2 41.3 %all-gather.14.cloned.1.call-done = bf16[8192,1024]{1,0:T(8,128)(2,1)} async-done(((bf16[8192,256]{1,0:T(8,128)(2,1)}), bf16[8192,1024]{1,0:T(8,128)(2,1)}) %all-gather.14.cloned.1.call-update) | async-done | bytes 16777232 | tf_op jit(solution)/shard_map/all_gather | solution.py:113
  343.5 12.7 %fusion.33 = f32[256]{0:T(256)S(1)} fusion(bf16[8192,1024]{1,0:T(8,128)(2,1)} %all-gather.14.cloned.1.call-done, bf16[256,128]{1,0:T(8,128)(2,1)S(1)} %convolution_convert_fusion, bf16[128,8192]{1,0:T(8,128)(2,1)} %all-gather.10.cloned.1.call-done, bf16[256,8192]{1,0:T(8,128)(2,1)} %bitcast.160, f32[8192]{0:T(1024)S(1)} %copy-done.11, ...), kind=kOutput, calls=%fused_computation.34 | convolution fusion | flops 4843372544 | bytes 23176192 | tf_op jit(solution)/shard_map/dot_general | solution.py:111
  (81 shorter events, 12.0 us)
Async XLA Ops:
  7.2 1.6 copy-start
  7.2 79.0 %all-gather.12.cloned.1.call-start = ((), (), s32[]{:S(2)}) async-start(), calls=%async_computation.5 | async-start | bytes 4718592 | tf_op jit(solution)/shard_map/all_gather | solution.py:110
  9.6 99.3 %all-gather.6.cloned.1.call-start = ((), (), s32[]{:S(2)}) async-start(), calls=%async_computation.2 | async-start | bytes 2621440 | tf_op jit(solution)/shard_map/all_gather | solution.py:56
  14.5 283.5 %all-gather.8.cloned.1.call-start = ((), (), s32[]{:S(2)}) async-start(), calls=%async_computation.3 | async-start | bytes 2359296 | tf_op jit(solution)/shard_map/all_gather | solution.py:96
  15.2 287.0 %all-gather.10.cloned.1.call-start = ((), (), s32[]{:S(2)}) async-start(), calls=%async_computation.4 | async-start | bytes 2359296 | tf_op jit(solution)/shard_map/all_gather | solution.py:102
  15.8 327.7 %all-gather.14.cloned.1.call-start = ((), (), s32[]{:S(2)}) async-start(), calls=%async_computation.6 | async-start | bytes 20971520 | tf_op jit(solution)/shard_map/all_gather | solution.py:113
  86.2 0.7 copy-start.8
  86.2 1.0 copy-start.7
  86.3 1.8 copy-start.9
  106.6 1.9 copy-start.10
  108.5 2.6 copy-start.3
  114.2 11.7 %copy-start.5 = (bf16[4,512,256]{2,1,0:T(8,128)(2,1)S(1)}, bf16[4,512,256]{2,1,0:T(8,128)(2,1)}, u32[]{:S(2)}) copy-start(bf16[4,512,256]{2,1,0:T(8,128)(2,1)} %get-tuple-element.299) | copy-start | bytes 3145732 | tf_op jit(solution)/shard_map/while
  128.0 11.7 %copy-start.5 = (bf16[4,512,256]{2,1,0:T(8,128)(2,1)S(1)}, bf16[4,512,256]{2,1,0:T(8,128)(2,1)}, u32[]{:S(2)}) copy-start(bf16[4,512,256]{2,1,0:T(8,128)(2,1)} %get-tuple-element.299) | copy-start | bytes 3145732 | tf_op jit(solution)/shard_map/while
  154.9 79.6 %all-to-all-start = ((bf16[8,128,4,256]{3,1,2,0:T(8,128)(2,1)}), bf16[8,128,4,256]{3,1,2,0:T(8,128)(2,1)}, u32[]{:S(2)}, u32[]{:S(2)}) async-start(bf16[8,128,4,256]{3,1,2,0:T(8,128)(2,1)} %fusion.42), calls=%async_computation | async-start | bytes 4194304 | tf_op jit(solution)/shard_map/all_to_all | solution.py:82
  162.3 11.7 %copy-start.6 = (bf16[4,512,256]{2,1,0:T(8,128)(2,1)S(1)}, bf16[4,512,256]{2,1,0:T(8,128)(2,1)}, u32[]{:S(2)}) copy-start(bf16[4,512,256]{2,1,0:T(8,128)(2,1)} %get-tuple-element.284) | copy-start | bytes 3145732 | tf_op jit(solution)/shard_map/while
  176.1 11.7 %copy-start.6 = (bf16[4,512,256]{2,1,0:T(8,128)(2,1)S(1)}, bf16[4,512,256]{2,1,0:T(8,128)(2,1)}, u32[]{:S(2)}) copy-start(bf16[4,512,256]{2,1,0:T(8,128)(2,1)} %get-tuple-element.284) | copy-start | bytes 3145732 | tf_op jit(solution)/shard_map/while
  203.0 36.9 %copy-start.4 = (bf16[4,4,128,256]{3,2,1,0:T(8,128)(2,1)S(1)}, bf16[4,4,128,256]{3,2,1,0:T(8,128)(2,1)}, u32[]{:S(2)}) copy-start(bf16[4,4,128,256]{3,2,1,0:T(8,128)(2,1)} %param.18) | copy-start | bytes 3145732
  203.0 37.5 %copy-start.2 = (s32[4,4]{1,0:T(4,128)S(1)}, s32[4,4]{1,0:T(4,128)}, u32[]{:S(2)}) copy-start(s32[4,4]{1,0:T(4,128)} %param.20) | copy-start | bytes 196
  234.5 52.2 %all-to-all-start.1 = ((bf16[8,128,4,256]{3,1,2,0:T(8,128)(2,1)}), bf16[8,128,4,256]{3,1,2,0:T(8,128)(2,1)}, u32[]{:S(2)}, u32[]{:S(2)}) async-start(bf16[8,128,4,256]{3,1,2,0:T(8,128)(2,1)} %fusion.34), calls=%async_computation.1 | async-start | bytes 4194304 | tf_op jit(solution)/shard_map/all_to_all | solution.py:82
  298.0 45.5 %copy-start.11 = (f32[8192]{0:T(1024)S(1)}, f32[8192]{0:T(1024)}, u32[]{:S(2)}) copy-start(f32[8192]{0:T(1024)} %param.27) | copy-start | bytes 98308
  298.0 45.5 %copy-start.12 = (f32[1024]{0:T(1024)S(1)}, f32[1024]{0:T(1024)}, u32[]{:S(2)}) copy-start(f32[1024]{0:T(1024)} %param.30) | copy-start | bytes 12292
  298.0 45.5 %copy-start.13 = (f32[1024]{0:T(1024)S(1)}, f32[1024]{0:T(1024)}, u32[]{:S(2)}) copy-start(f32[1024]{0:T(1024)} %param.29) | copy-start | bytes 12292
  343.5 13.3 %copy-start.1 = (bf16[1024,1024]{1,0:T(8,128)(2,1)S(1)}, bf16[1024,1024]{1,0:T(8,128)(2,1)}, u32[]{:S(2)}) copy-start(bf16[1024,1024]{1,0:T(8,128)(2,1)} %param.28) | copy-start | bytes 6291460
Sparse Core Ops, SparseCore 0:
  10.7 75.4 all-gather.11
  87.8 21.0 all-gather.5
  111.1 49.1 all-gather.7
  162.3 74.1 all-gather.9
  237.9 105.5 all-gather.13
